TPU v7x, 128 devices: a whole 4x4x4 slice. The times are simulated.
128 devices in a mesh: row: 16 (over z_lo, x, core), col: 8 (over y, z_hi).
Axes of the slice: x: 4, y: 4, z: 4 (z_hi: 2, z_lo: 2; z = z_hi * 2 + z_lo), core: 2. Of those that a mesh axis runs over, the one named last changes fastest.
Arguments:
- amplitudes: bfloat16 [7168, 7168], P('row', 'col'), as said below
- integrals: bfloat16 [7168, 7168], P('row', 'col'), as said below
- occ_energy: float32 [80], replicated, may hold values from -2 to -0.5
- vir_energy: float32 [1000], replicated, may hold values from 0.5 to 4
- pair_occ: int32 [7168], replicated, may hold values from 0 to 79, as said below
- pair_vir: int32 [7168], replicated, may hold values from 0 to 999, as said below
Outputs:
- updated: float32 [7168, 7168], P('row', 'col')
Inputs may be any that keep to these rules, and one draw needn't show every extreme that they name: amplitudes is exactly symmetric. integrals is exactly symmetric. pair_occ[p] mod 8 equals pair_vir[p] mod 8 (one irrep block), and no pair (pair_occ[p], pair_vir[p]) occurs twice. `pair_vir`: see pair_occ.
All inputs are finite; a program needn't handle non-finite values.
Results may differ from a plain program's by a relative error of at most 0.0003.
Values may be sent and summed in bfloat16 or wider, within the bound.
No kernel may reach another device: no remote copies, remote signals or barrier semaphores. Data moves between devices by JAX's collectives and lax.ppermute only.
A program may use at most 128 MiB of HBM per device.

v0:
```python
import jax
import jax.numpy as jnp
from jax import lax
from jax.sharding import PartitionSpec as P


def lookup(energies, orbital_index):
    labels = jnp.arange(energies.shape[0], dtype=jnp.int32)
    picked = jnp.where(orbital_index[:, None] == labels[None, :], energies[None, :], 0.0)
    return jnp.sum(picked, axis=1)


def shards(amplitudes, integrals, occ_energy, vir_energy, pair_occ, pair_vir):
    tile_rows, tile_cols = amplitudes.shape
    left_local = jnp.stack((amplitudes, integrals))
    right_local = jnp.stack((integrals, amplitudes))
    row_panels = lax.all_gather(left_local, "col", axis=2, tiled=True)
    summed = jnp.einsum(
        "lrk,lkc->rc",
        row_panels,
        lax.all_gather(right_local, "row", axis=1, tiled=True),
        preferred_element_type=jnp.float32,
    )
    row_start = lax.axis_index("row") * tile_rows
    col_start = lax.axis_index("col") * tile_cols
    row_occ = lax.dynamic_slice_in_dim(pair_occ, row_start, tile_rows)
    row_vir = lax.dynamic_slice_in_dim(pair_vir, row_start, tile_rows)
    col_occ = lax.dynamic_slice_in_dim(pair_occ, col_start, tile_cols)
    col_vir = lax.dynamic_slice_in_dim(pair_vir, col_start, tile_cols)
    row_gap = lookup(occ_energy, row_occ) - lookup(vir_energy, row_vir)
    col_gap = lookup(occ_energy, col_occ) - lookup(vir_energy, col_vir)
    return summed / (row_gap[:, None] + col_gap[None, :])


def solution(mesh):
    return jax.shard_map(
        shards,
        mesh=mesh,
        in_specs=(P("row", "col"), P("row", "col"), P(), P(), P(), P()),
        out_specs=P("row", "col"),
        check_vma=False,
    )
```

profile of v0, /device:TPU:1, one launch (start us, length us, event | category | flops | bytes accessed | tf_op | source)
XLA Modules:
  0.0 323.7 jit_solution(3779648207988396233)
XLA Ops:
  6.5 0.0 all-gather.3.cloned.1.call-start
  6.5 4.0 %pad_maximum_fusion.1 = (bf16[2,448,896]{2,1,0:T(8,128)(2,1)}, bf16[2,448,896]{2,1,0:T(8,128)(2,1)}) fusion(bf16[1,448,896]{2,1,0:T(8,128)(2,1)} %bitcast.6, bf16[1,448,896]{2,1,0:T(8,128)(2,1)} %bitcast.7), kind=kLoop, calls=%fused_computation.5 | loop fusion | flops 1605632 | bytes 4816896 | tf_op jit(solution)/shard_map/stack | solution.py:16
  10.5 0.0 copy-start.1
  10.5 0.0 copy-start
  10.5 0.0 all-gather.3.cloned.1.call-update
  10.5 0.0 all-gather.5.cloned.1.call-start
  10.6 0.7 all-gather.5.cloned.1.call-update
  11.3 0.8 dynamic_slice.14
  12.1 0.8 dynamic_slice.15
  12.9 0.8 dynamic_slice.12
  13.6 0.8 dynamic_slice.13
  14.4 0.0 copy-done.1
  14.4 0.1 select_reduce_fusion.2
  14.5 0.0 copy-done
  14.5 0.5 select_reduce_fusion
  15.0 0.1 select_reduce_fusion.3
  15.1 0.3 select_reduce_fusion.1
  15.5 146.1 %all-gather.3.cloned.1.call-done = bf16[2,448,7168]{2,1,0:T(8,128)(2,1)} async-done(((bf16[2,448,896]{2,1,0:T(8,128)(2,1)}), bf16[2,448,7168]{2,1,0:T(8,128)(2,1)}) %all-gather.3.cloned.1.call-update) | async-done | bytes 12845072 | tf_op jit(solution)/shard_map/all_gather | solution.py:17
  161.6 133.8 %all-gather.5.cloned.1.call-done = bf16[2,7168,896]{2,1,0:T(8,128)(2,1)} async-done(((bf16[2,448,896]{2,1,0:T(8,128)(2,1)}), bf16[2,7168,896]{2,1,0:T(8,128)(2,1)}) %all-gather.5.cloned.1.call-update) | async-done | bytes 25690128 | tf_op jit(solution)/shard_map/all_gather | solution.py:21
  295.4 21.5 %bitcast_divide_fusion = f32[448,896]{1,0:T(8,128)} fusion(bf16[2,448,7168]{2,1,0:T(8,128)(2,1)} %all-gather.3.cloned.1.call-done, bf16[2,7168,896]{2,1,0:T(8,128)(2,1)} %all-gather.5.cloned.1.call-done, f32[896]{0:T(1024)S(1)} %sub.15, f32[448]{0:T(512)S(1)} %sub.14), kind=kOutput, calls=%fused_computation.6 | convolution fusion | flops 11509972992 | bytes 40146176 | tf_op jit(solution)/shard_map/lrk,lkc->rc/dot_general | solution.py:18
  (2 shorter events, 0.0 us)
Async XLA Ops:
  6.5 155.0 %all-gather.3.cloned.1.call-start = ((), (), s32[]{:S(2)}) async-start(), calls=%async_computation | async-start | bytes 14450688 | tf_op jit(solution)/shard_map/all_gather | solution.py:17
  10.5 3.9 %copy-start.1 = (f32[80]{0:T(128)S(1)}, f32[80]{0:T(128)}, u32[]{:S(2)}) copy-start(f32[80]{0:T(128)} %param.8) | copy-start | bytes 964
  10.5 4.0 %copy-start = (f32[1000]{0:T(1024)S(1)}, f32[1000]{0:T(1024)}, u32[]{:S(2)}) copy-start(f32[1000]{0:T(1024)} %param.9) | copy-start | bytes 12004
  10.5 284.8 %all-gather.5.cloned.1.call-start = ((), (), s32[]{:S(2)}) async-start(), calls=%async_computation.1 | async-start | bytes 27295744 | tf_op jit(solution)/shard_map/all_gather | solution.py:21
Sparse Core Ops, SparseCore 0:
  10.7 150.8 all-gather.2
  163.2 132.1 all-gather.4
where the time goes:
time: 324 us
  waiting for transfers between devices  281 us (87%)
  matrix products  21.5 us (7%)
  between operations  13.4 us (4%)
  other arithmetic  5.01 us (2%)
    all_gather x1, waiting for transfers between devices, shards(): row_panels = lax.all_gather(left_local, 'col', axis=2, tiled=True)  146 us
    all_gather x1, waiting for transfers between devices, shards(): lax.all_gather(right_local, 'row', axis=1, tiled=True)  134 us
    dot_general x1, matrix products, shards(): jnp.einsum('lrk,lkc->rc', row_panels, lax.all_gather(right_local, 'row',...  21.5 us
  transfers between devices with their start and end apart: 2, of which 2 were waited for; matrix products, arithmetic and copies ran while one was open for 1% of the time, Pallas kernels for 0%

commit v1 on v0

--- a/solution.py
+++ b/solution.py
@@ -2,6 +2,16 @@
 import jax.numpy as jnp
 from jax import lax
 from jax.sharding import PartitionSpec as P
+
+
+def play_notes_up(my_data):
+    low = jax.lax.all_to_all(
+        jnp.stack([my_data for _ in range(jax.lax.axis_size("row"))], 0),
+        axis_name="row",
+        split_axis=0,
+        concat_axis=0,
+    )
+    return jnp.concatenate(low, axis=1)
 
 
 def lookup(energies, orbital_index):
@@ -16,10 +26,7 @@
     right_local = jnp.stack((integrals, amplitudes))
     row_panels = lax.all_gather(left_local, "col", axis=2, tiled=True)
     summed = jnp.einsum(
-        "lrk,lkc->rc",
-        row_panels,
-        lax.all_gather(right_local, "row", axis=1, tiled=True),
-        preferred_element_type=jnp.float32,
+        "lrk,lkc->rc", row_panels, play_notes_up(right_local), preferred_element_type=jnp.float32
     )
     row_start = lax.axis_index("row") * tile_rows
     col_start = lax.axis_index("col") * tile_cols

time: 324 us -> 445 us (1.37)
  waiting for transfers between devices: 281 us -> 365 us
  local copies, waits for them, and re-layouts: 3.1 us -> 32.6 us
  starting transfers between devices: 0.04 us -> 7.34 us
    all_to_all x0 -> x1, waiting for transfers between devices: none -> 340 us  [play_notes_up(): jax.lax.all_to_all(jnp.stack([my_data for _ in range(jax.lax.axis_size('r...]
    all_gather x1 -> x0, waiting for transfers between devices: 134 us -> none  [shards(): lax.all_gather(right_local, 'row', axis=1, tiled=True)]
    all_gather x1, waiting for transfers between devices: 146 us -> 24.5 us  [shards(): row_panels = lax.all_gather(left_local, 'col', axis=2, tiled=True)]
    reshape x0 -> x1, local copies, waits for them, and re-layouts: none -> 21 us  [play_notes_up(): return jnp.concatenate(low, axis=1)]
    another operation x0 -> x1, local copies, waits for them, and re-layouts: none -> 8.56 us  [play_notes_up(): jnp.stack([my_data for _ in range(jax.lax.axis_size('row'))], 0)]
    all_to_all x0 -> x1, starting transfers between devices: none -> 7.3 us  [play_notes_up(): jax.lax.all_to_all(jnp.stack([my_data for _ in range(jax.lax.axis_size('r...]
  transfers between devices with their start and end apart: 2 -> 2, of which waited for: 2 -> 2; matrix products, arithmetic and copies ran while one was open for 1% -> 6% of each run, Pallas kernels for 0% -> 0%
where the time goes in v1:
time: 445 us; the launch traced here: 444 us
  waiting for transfers between devices  365 us (82%)
  local copies, waits for them, and re-layouts  32.6 us (7%)
  matrix products  21.6 us (5%)
  between operations  13.4 us (3%)
  starting transfers between devices  7.34 us (2%)
    all_to_all x1, waiting for transfers between devices, play_notes_up(): jax.lax.all_to_all(jnp.stack([my_data for _ in range(jax.lax.axis_size('r...  340 us
    all_gather x1, waiting for transfers between devices, shards(): row_panels = lax.all_gather(left_local, 'col', axis=2, tiled=True)  24.5 us
    dot_general x1, matrix products, shards(): jnp.einsum('lrk,lkc->rc', row_panels, play_notes_up(right_local), preferr...  21.6 us
    reshape x1, local copies, waits for them, and re-layouts, play_notes_up(): return jnp.concatenate(low, axis=1)  21 us
  transfers between devices with their start and end apart: 2, of which 2 were waited for; matrix products, arithmetic and copies ran while one was open for 6% of the time, Pallas kernels for 0%

profile of v1, /device:TPU:1, one launch (start us, length us, event | category | flops | bytes accessed | tf_op | source)
XLA Modules:
  0.0 444.4 jit_solution(6157308351587136310)
XLA Ops:
  6.5 3.4 pad_maximum_fusion.1
  9.9 8.6 %stack.14 = bf16[16,2,448,896]{3,2,1,0:T(8,128)(2,1)} broadcast(bf16[2,448,896]{2,1,0:T(8,128)(2,1)S(1)} %get-tuple-element.5), dimensions={1,2,3} | broadcast | bytes 27295744 | tf_op jit(solution)/shard_map/stack | solution.py:9
  18.5 0.0 copy-start.1
  18.5 0.0 copy-start
  18.5 7.3 %all-to-all-start = ((bf16[16,2,448,896]{3,2,1,0:T(8,128)(2,1)}), bf16[16,2,448,896]{3,2,1,0:T(8,128)(2,1)}, u32[]{:S(2)}, u32[]{:S(2)}) async-start(bf16[16,2,448,896]{3,2,1,0:T(8,128)(2,1)} %stack.14), calls=%async_computation | async-start | bytes 51380224 | tf_op jit(solution)/shard_map/all_to_all | solution.py:8
  25.8 0.0 all-gather.2.cloned.1.call-start
  25.9 0.7 all-gather.2.cloned.1.call-update
  26.6 0.8 dynamic_slice.15
  27.3 0.8 dynamic_slice.14
  28.1 0.8 dynamic_slice.13
  28.9 0.8 dynamic_slice.12
  29.6 0.0 copy-done.1
  29.6 0.1 select_reduce_fusion.2
  29.8 0.0 copy-done
  29.8 0.5 select_reduce_fusion
  30.3 0.1 select_reduce_fusion.3
  30.4 0.3 select_reduce_fusion.1
  30.7 339.7 %all-to-all-done = bf16[16,2,448,896]{3,2,1,0:T(8,128)(2,1)} async-done(((bf16[16,2,448,896]{3,2,1,0:T(8,128)(2,1)}), bf16[16,2,448,896]{3,2,1,0:T(8,128)(2,1)}, u32[]{:S(2)}, u32[]{:S(2)}) %all-to-all-start) | async-done | bytes 25690144 | tf_op jit(solution)/shard_map/all_to_all | solution.py:8
  370.4 21.0 %copy.8 = bf16[2,16,448,896]{3,2,1,0:T(8,128)(2,1)} copy(bf16[2,16,448,896]{3,2,0,1:T(8,128)(2,1)} %bitcast.2) | data formatting | bytes 51380224 | tf_op jit(solution)/shard_map/reshape | solution.py:14
  391.4 24.5 %all-gather.2.cloned.1.call-done = bf16[2,448,7168]{2,1,0:T(8,128)(2,1)} async-done(((bf16[2,448,896]{2,1,0:T(8,128)(2,1)}), bf16[2,448,7168]{2,1,0:T(8,128)(2,1)}) %all-gather.2.cloned.1.call-update) | async-done | bytes 12845072 | tf_op jit(solution)/shard_map/all_gather | solution.py:27
  415.9 21.6 %bitcast_divide_fusion = f32[448,896]{1,0:T(8,128)} fusion(bf16[2,448,7168]{2,1,0:T(8,128)(2,1)} %all-gather.2.cloned.1.call-done, bf16[2,7168,896]{2,1,0:T(8,128)(2,1)} %bitcast.8, f32[896]{0:T(1024)S(1)} %sub.15, f32[448]{0:T(512)S(1)} %sub.14), kind=kOutput, calls=%fused_computation.6 | convolution fusion | flops 11509972992 | bytes 40146176 | tf_op jit(solution)/shard_map/lrk,lkc->rc/dot_general | solution.py:28
  (2 shorter events, 0.0 us)
Async XLA Ops:
  18.5 11.1 %copy-start.1 = (f32[80]{0:T(128)S(1)}, f32[80]{0:T(128)}, u32[]{:S(2)}) copy-start(f32[80]{0:T(128)} %param.8) | copy-start | bytes 964
  18.5 11.3 %copy-start = (f32[1000]{0:T(1024)S(1)}, f32[1000]{0:T(1024)}, u32[]{:S(2)}) copy-start(f32[1000]{0:T(1024)} %param.9) | copy-start | bytes 12004
  18.5 351.9 %all-to-all-start = ((bf16[16,2,448,896]{3,2,1,0:T(8,128)(2,1)}), bf16[16,2,448,896]{3,2,1,0:T(8,128)(2,1)}, u32[]{:S(2)}, u32[]{:S(2)}) async-start(bf16[16,2,448,896]{3,2,1,0:T(8,128)(2,1)} %stack.14), calls=%async_computation | async-start | bytes 51380224 | tf_op jit(solution)/shard_map/all_to_all | solution.py:8
  25.8 390.1 %all-gather.2.cloned.1.call-start = ((), (), s32[]{:S(2)}) async-start(), calls=%async_computation.1 | async-start | bytes 14450688 | tf_op jit(solution)/shard_map/all_gather | solution.py:27
Sparse Core Ops, SparseCore 0:
  29.0 386.8 all-gather.1
